TPU v7x, 32 devices: a whole 2x2x4 slice. The times are simulated.
32 devices in a mesh: groups: 2 (over y), seq: 4 (over z), section: 2 (over x), chan: 2 (over core).
Axes of the slice: x: 2, y: 2, z: 4, core: 2. Of those that a mesh axis runs over, the one named last changes fastest.
Arguments:
- base_codes: int32 [131072], P(('groups', 'seq', 'section')), parts along dimension 0, may hold values from 0 to 3
- stem_weight: bfloat16 [64, 768], replicated, as said below
- conv_gain: float32 [768], replicated, may hold values from 0.1 to 1.9
- dilated_conv_weight: bfloat16 [3, 768, 768], P(None, None, 'chan'), may hold values from -0.125 to 0.125
- widen_weight: bfloat16 [768, 1536], P(None, 'chan'), may hold values from -0.21875 to 0.21875
- token_gain: float32 [1536], replicated, may hold values from 0.1 to 1.9
- proj_weight: bfloat16 [1536, 256], replicated, may hold values from -0.15625 to 0.15625
- dist_weight: float32 [128], replicated, may hold values from -4 to 4
- pair_weight_one: bfloat16 [3, 3, 128, 128], P(None, None, None, 'chan'), may hold values from -0.1875 to 0.1875
- pair_weight_two: bfloat16 [3, 3, 128, 128], P(None, None, None, 'chan'), may hold values from -0.1875 to 0.1875
Outputs:
- fine_features: bfloat16 [4096, 1536], P(('groups', 'seq', 'section'), 'chan'), parts along dimension 0
- pair_map: bfloat16 [128, 64, 32], P('chan', ('groups', 'seq'), 'section'), parts along dimension 1
There are 2 independent parts, one for each index of `groups`. A program takes and returns all parts, laid end to end along the dimension named above; an argument that names none is the same for every part. Nothing has to cross between parts.
Inputs may be any that keep to these rules, and one draw needn't show every extreme that they name: Each entry of stem_weight is under 9 / sqrt(16) in magnitude.
All inputs are finite; a program needn't handle non-finite values.
Results may differ from a plain program's by a relative error of at most 0.015.
Values may be sent and summed in bfloat16 or wider, within the bound.
No kernel may reach another device: no remote copies, remote signals or barrier semaphores. Data moves between devices by JAX's collectives and lax.ppermute only.
A program may use at most 64 MiB of HBM per device.

v0:
```python
import math
import jax
import jax.numpy as jnp
from jax import lax
from jax.sharding import PartitionSpec as P

PC = 128
PATCH = 16
POOL = 64
DILATION_ROWS = 4
epsilon = 1e-06


def padded(cells, sides, width):
    for axis, dim in sides:
        count = lax.axis_size(axis)
        ends = count - 1
        head = lax.slice_in_dim(cells, 0, width, axis=dim)
        tail = lax.slice_in_dim(cells, cells.shape[dim] - width, cells.shape[dim], axis=dim)
        cells = jnp.concatenate(
            [
                lax.ppermute(tail, axis, [(i, (i + 1) % count) for i in range(ends)]),
                cells,
                lax.ppermute(head, axis, [((i + 1) % count, i) for i in range(ends)]),
            ],
            axis=dim,
        )
    return cells


def row_norm(values, gain):
    mean_square = jnp.mean(values * values, axis=1, keepdims=True)
    return values * lax.rsqrt(mean_square + epsilon) * gain


def pair_conv(active, weight):
    row_len = active.shape[1] - 2
    col_len = active.shape[2] - 2
    total = jnp.zeros((weight.shape[3], row_len, col_len), jnp.float32)
    for shift_row in range(3):
        for shift_col in range(3):
            window = active[:, shift_row : shift_row + row_len, shift_col : shift_col + col_len]
            total = total + jnp.einsum(
                "co,crs->ors",
                weight[shift_row, shift_col],
                window,
                preferred_element_type=jnp.float32,
            )
    return total


def make_pair(row_factor, col_factor, row_index, col_index, dist_weight, tokens_total):
    gap = jnp.abs(row_index[:, None] - col_index[None, :]).astype(jnp.float32)
    distance = jnp.log1p(gap) / math.log(tokens_total)
    product = (
        row_factor.astype(jnp.float32).T[:, :, None] * col_factor.astype(jnp.float32).T[:, None, :]
    )
    return product + dist_weight[:, None, None] * distance[None, :, :]


def per_device(
    base_codes,
    stem_weight,
    conv_gain,
    dilated_conv_weight,
    widen_weight,
    token_gain,
    proj_weight,
    dist_weight,
    pair_weight_one,
    pair_weight_two,
):
    count_of_rows = base_codes.shape[0] // PATCH
    coded = base_codes.reshape(count_of_rows, PATCH)
    onehot = (
        (coded[:, :, None] == jnp.arange(4, dtype=jnp.int32)[None, None, :])
        .astype(jnp.bfloat16)
        .reshape(count_of_rows, 4 * PATCH)
    )
    half_width = dilated_conv_weight.shape[2]
    own_index = lax.axis_index("chan")
    weight_own = lax.dynamic_slice_in_dim(stem_weight, own_index * half_width, half_width, 1)
    stem_own = jnp.dot(onehot, weight_own, preferred_element_type=jnp.float32).astype(jnp.bfloat16)
    full_stem_output = lax.all_gather(stem_own, "chan", axis=1, tiled=True)
    padded_rows = padded(full_stem_output, ((("seq", "section"), 0),), DILATION_ROWS)
    normalized_rows = row_norm(padded_rows.astype(jnp.float32), conv_gain).astype(jnp.bfloat16)
    summed_taps = jnp.zeros((count_of_rows, half_width), jnp.float32)
    for row_shift_amount in range(3):
        summed_taps = summed_taps + jnp.dot(
            normalized_rows[
                row_shift_amount * DILATION_ROWS : row_shift_amount * DILATION_ROWS + count_of_rows
            ],
            dilated_conv_weight[row_shift_amount],
            preferred_element_type=jnp.float32,
        )
    tower = (stem_own.astype(jnp.float32) + jax.nn.gelu(summed_taps)).astype(jnp.bfloat16)
    halved = jnp.maximum(tower[0::2], tower[1::2])
    widened = jnp.dot(
        lax.all_gather(halved, "chan", axis=1, tiled=True),
        widen_weight,
        preferred_element_type=jnp.float32,
    )
    fine_features = jax.nn.gelu(widened).astype(jnp.bfloat16)
    tok_count = fine_features.shape[0] // POOL
    token = jnp.mean(
        fine_features.astype(jnp.float32).reshape(tok_count, POOL, fine_features.shape[1]), axis=1
    ).astype(jnp.bfloat16)
    token_full = lax.all_gather(token, "chan", axis=1, tiled=True)
    token_norm = row_norm(token_full.astype(jnp.float32), token_gain).astype(jnp.bfloat16)
    factors = jnp.dot(token_norm, proj_weight, preferred_element_type=jnp.float32).astype(
        jnp.bfloat16
    )
    seq_count = lax.axis_size("seq")
    section_count = lax.axis_size("section")
    tokens_total = tok_count * seq_count * section_count
    tile_height = tok_count * section_count
    tile_width = tok_count * seq_count
    row_anchor = lax.axis_index("seq") * tile_height
    col_anchor = lax.axis_index("section") * tile_width
    pair_own = pair_weight_one.shape[3]
    every_token = lax.all_gather(factors, ("seq", "section"), axis=0, tiled=True)
    zero_padded = jnp.pad(every_token, ((1, 1), (0, 0)))
    row_factor = lax.dynamic_slice_in_dim(zero_padded, row_anchor, tile_height + 2, 0)[:, :PC]
    col_factor = lax.dynamic_slice_in_dim(zero_padded, col_anchor, tile_width + 2, 0)[:, PC:]
    row_index = row_anchor - 1 + jnp.arange(tile_height + 2, dtype=jnp.int32)
    col_index = col_anchor - 1 + jnp.arange(tile_width + 2, dtype=jnp.int32)
    extended = make_pair(
        row_factor, col_factor, row_index, col_index, dist_weight, tokens_total
    ).astype(jnp.bfloat16)
    row_valid = (row_index >= 0) & (row_index < tokens_total)
    col_valid = (col_index >= 0) & (col_index < tokens_total)
    inside = row_valid[:, None] & col_valid[None, :]
    act_one = jnp.where(inside[None, :, :], jax.nn.gelu(extended.astype(jnp.float32)), 0.0).astype(
        jnp.bfloat16
    )
    pair_start = extended[:, 1:-1, 1:-1]
    start_own = lax.dynamic_slice_in_dim(pair_start, own_index * pair_own, pair_own, 0)
    pair_mid = (start_own.astype(jnp.float32) + pair_conv(act_one, pair_weight_one)).astype(
        jnp.bfloat16
    )
    mid_full = lax.all_gather(pair_mid, "chan", axis=0, tiled=True)
    act_local_two = jax.nn.gelu(mid_full.astype(jnp.float32)).astype(jnp.bfloat16)
    act_two = padded(act_local_two, (("seq", 1), ("section", 2)), 1)
    pair_map = (pair_mid.astype(jnp.float32) + pair_conv(act_two, pair_weight_two)).astype(
        jnp.bfloat16
    )
    return (fine_features, pair_map)


def solution(mesh):
    in_specs = (
        P(("groups", "seq", "section")),
        P(),
        P(),
        P(None, None, "chan"),
        P(None, "chan"),
        P(),
        P(),
        P(),
        P(None, None, None, "chan"),
        P(None, None, None, "chan"),
    )
    out_specs = (P(("groups", "seq", "section"), "chan"), P("chan", ("groups", "seq"), "section"))
    return jax.shard_map(
        per_device, mesh=mesh, in_specs=in_specs, out_specs=out_specs, check_vma=False
    )
```

profile of v0, /device:TPU:0, one launch (start us, length us, event | category | flops | bytes accessed | tf_op | source)
XLA Modules:
  0.0 73.8 jit_solution(9603304205572424095)
XLA Ops:
  0.7 1.0 %eq.22 = s32[512,16]{1,0:T(8,128)S(1)} reshape(s32[8192]{0:T(1024)} %param.10) | data formatting | bytes 65536 | tf_op jit(solution)/shard_map/eq | solution.py:76
  1.9 1.2 %convolution_convert_fusion = bf16[512,384]{1,0:T(8,128)(2,1)S(1)} fusion(s32[512,64]{0,1:T(8,128)S(1)} %eq.24, s32[64]{0:T(128)S(1)} %eq.26, bf16[64,768]{1,0:T(8,128)(2,1)} %param.11, s32[]{:T(128)S(6)} %select_n.16), kind=kOutput, calls=%fused_computation.7 | convolution fusion | flops 25395200 | bytes 573700 | tf_op jit(solution)/shard_map/dot_general | solution.py:83
  3.1 2.5 %all_gather.15 = bf16[512,768]{1,0:T(8,128)(2,1)S(1)} all-gather(bf16[512,384]{1,0:T(8,128)(2,1)S(1)} %convolution_convert_fusion), channel_id=1, replica_groups=mesh['groups'=2,'seq'=4,'section'=2,'chan'=2] {'chan'}, dimensions={1}, use_global_device_ids=true | all-gather | bytes 1179648 | tf_op jit(solution)/shard_map/all_gather | solution.py:84
  5.6 4.8 %collective-permute-start = (bf16[4,768]{1,0:T(4,128)(2,1)S(1)}, bf16[4,768]{1,0:T(4,128)(2,1)S(1)}, u32[]{:S(2)}, u32[]{:S(2)}) collective-permute-start(bf16[4,768]{1,0:T(4,128)(2,1)S(1)} %get-tuple-element.4), channel_id=1, source_target_pairs={{0,2},{2,4},{4,6},{6,8},{8,10},{10,12},{12,14},{1,3},{3,5},{5,7},{... | collective-permute-start | bytes 18440 | tf_op jit(solution)/shard_map/ppermute | solution.py:22
  10.4 1.3 %collective-permute-start.1 = (bf16[4,768]{1,0:T(4,128)(2,1)S(1)}, bf16[4,768]{1,0:T(4,128)(2,1)S(1)}, u32[]{:S(2)}, u32[]{:S(2)}) collective-permute-start(bf16[4,768]{1,0:T(4,128)(2,1)S(1)} %get-tuple-element.5), channel_id=1, source_target_pairs={{2,0},{4,2},{6,4},{8,6},{10,8},{12,10},{14,12},{3,1},{5,3},{7,5},{... | collective-permute-start | bytes 18440 | tf_op jit(solution)/shard_map/ppermute | solution.py:24
  11.9 4.0 %collective-permute-done.1 = bf16[4,768]{1,0:T(4,128)(2,1)S(1)} collective-permute-done((bf16[4,768]{1,0:T(4,128)(2,1)S(1)}, bf16[4,768]{1,0:T(4,128)(2,1)S(1)}, u32[]{:S(2)}, u32[]{:S(2)}) %collective-permute-start.1) | collective-permute-done | bytes 6176 | tf_op jit(solution)/shard_map/ppermute | solution.py:24
  15.9 0.3 fusion
  16.3 0.3 fusion.2
  16.6 0.6 fusion.34
  17.2 0.6 convolution_add_fusion.1
  17.8 0.8 %fusion.24 = bf16[512,384]{1,0:T(8,128)(2,1)S(1)} fusion(f32[512,384]{1,0:T(8,128)S(1)} %convolution_add_fusion.1, bf16[520,768]{1,0:T(8,128)(2,1)S(1)} %fusion.2, bf16[512,384]{1,0:T(8,128)(2,1)S(1)} %convolution_convert_fusion, bf16[3,768,384]{2,1,0:T(8,128)(2,1)S(1)} %copy-done.2), kind=kOutput, calls=%fused_computation.43 | convolution fusion | flops 304349184 | bytes 2949120 | tf_op jit(solution)/shard_map/dot_general | solution.py:89
  18.6 0.6 slice.172
  19.2 0.6 slice.173
  19.8 2.1 %all_gather.16 = bf16[256,768]{1,0:T(8,128)(2,1)S(1)} all-gather(bf16[256,384]{1,0:T(8,128)(2,1)S(1)} %max.3), channel_id=1, replica_groups=mesh['groups'=2,'seq'=4,'section'=2,'chan'=2] {'chan'}, dimensions={1}, use_global_device_ids=true | all-gather | bytes 589824 | tf_op jit(solution)/shard_map/all_gather | solution.py:99
  21.9 1.4 %convert_reduce_fusion = (f32[4,768]{1,0:T(4,128)S(1)}, bf16[256,768]{1,0:T(8,128)(2,1)}) fusion(bf16[256,768]{1,0:T(8,128)(2,1)S(1)} %all_gather.16, bf16[768,768]{1,0:T(8,128)(2,1)S(1)} %copy-done), kind=kOutput, calls=%fused_computation.56 | convolution fusion | flops 304149504 | bytes 1978368 | tf_op jit(solution)/shard_map/dot_general | solution.py:98
  23.3 1.8 %all_gather.17 = bf16[4,1536]{1,0:T(4,128)(2,1)S(1)} all-gather(bf16[4,768]{1,0:T(4,128)(2,1)S(1)} %multiply_convert_fusion), channel_id=1, replica_groups=mesh['groups'=2,'seq'=4,'section'=2,'chan'=2] {'chan'}, dimensions={1}, use_global_device_ids=true | all-gather | bytes 18432 | tf_op jit(solution)/shard_map/all_gather | solution.py:108
  25.3 0.2 fusion.15
  25.5 26.6 %all-gather = bf16[8,4,256]{2,1,0:T(4,128)(2,1)S(1)} all-gather(bf16[1,4,256]{2,1,0:T(4,128)(2,1)S(1)} %fusion.15), channel_id=1, replica_groups=mesh['groups'=2,'seq'=4,'section'=2,'chan'=2] {'seq','section'}, dimensions={0}, use_global_device_ids=true | all-gather | bytes 18432 | tf_op jit(solution)/shard_map/all_gather | solution.py:121
  52.5 0.1 convolution_add_fusion.11
  53.0 0.1 convolution_add_fusion.8
  53.4 0.1 convolution_add_fusion.5
  53.8 2.0 %all_gather.19 = bf16[128,8,16]{2,1,0:T(8,128)(2,1)S(1)} all-gather(bf16[64,8,16]{2,1,0:T(8,128)(2,1)S(1)} %copy.17), channel_id=1, replica_groups=mesh['groups'=2,'seq'=4,'section'=2,'chan'=2] {'chan'}, dimensions={0}, use_global_device_ids=true | all-gather | bytes 49152 | tf_op jit(solution)/shard_map/all_gather | solution.py:141
  55.8 0.2 copy.18
  56.1 2.2 %collective-permute-start.2 = (bf16[128,1,16]{0,2,1:T(8,128)(2,1)S(1)}, bf16[128,1,16]{0,2,1:T(8,128)(2,1)S(1)}, u32[]{:S(2)}, u32[]{:S(2)}) collective-permute-start(bf16[128,1,16]{0,2,1:T(8,128)(2,1)S(1)} %get-tuple-element.10), channel_id=1, source_target_pairs={{0,4},{4,8},{8,12},{1,5},{5,9},{9,13},{2,6},{6,10},{10,14},{3,7},{... | collective-permute-start | bytes 12296 | tf_op jit(solution)/shard_map/ppermute | solution.py:22
  58.3 1.3 %collective-permute-start.3 = (bf16[128,1,16]{0,2,1:T(8,128)(2,1)S(1)}, bf16[128,1,16]{0,2,1:T(8,128)(2,1)S(1)}, u32[]{:S(2)}, u32[]{:S(2)}) collective-permute-start(bf16[128,1,16]{0,2,1:T(8,128)(2,1)S(1)} %get-tuple-element.11), channel_id=1, source_target_pairs={{4,0},{8,4},{12,8},{5,1},{9,5},{13,9},{6,2},{10,6},{14,10},{7,3},{... | collective-permute-start | bytes 12296 | tf_op jit(solution)/shard_map/ppermute | solution.py:24
  59.6 0.1 fusion.94
  59.7 4.0 %collective-permute-done.3 = bf16[128,1,16]{0,2,1:T(8,128)(2,1)S(1)} collective-permute-done((bf16[128,1,16]{0,2,1:T(8,128)(2,1)S(1)}, bf16[128,1,16]{0,2,1:T(8,128)(2,1)S(1)}, u32[]{:S(2)}, u32[]{:S(2)}) %collective-permute-start.3) | collective-permute-done | bytes 4128 | tf_op jit(solution)/shard_map/ppermute | solution.py:24
  63.8 3.0 %collective-permute-start.4 = (bf16[128,10,1]{0,2,1:T(2,128)(2,1)S(1)}, bf16[128,10,1]{0,2,1:T(2,128)(2,1)S(1)}, u32[]{:S(2)}, u32[]{:S(2)}) collective-permute-start(bf16[128,10,1]{0,2,1:T(2,128)(2,1)S(1)} %get-tuple-element.8), channel_id=1, source_target_pairs={{0,2},{1,3},{4,6},{5,7},{8,10},{9,11},{12,14},{13,15},{16,18},{17,... | collective-permute-start | bytes 7688 | tf_op jit(solution)/shard_map/ppermute | solution.py:22
  66.8 1.3 %collective-permute-start.5 = (bf16[128,10,1]{0,2,1:T(2,128)(2,1)S(1)}, bf16[128,10,1]{0,2,1:T(2,128)(2,1)S(1)}, u32[]{:S(2)}, u32[]{:S(2)}) collective-permute-start(bf16[128,10,1]{0,2,1:T(2,128)(2,1)S(1)} %get-tuple-element.9), channel_id=1, source_target_pairs={{2,0},{3,1},{6,4},{7,5},{10,8},{11,9},{14,12},{15,13},{18,16},{19,... | collective-permute-start | bytes 7688 | tf_op jit(solution)/shard_map/ppermute | solution.py:24
  68.4 4.0 %collective-permute-done.5 = bf16[128,10,1]{0,2,1:T(2,128)(2,1)S(1)} collective-permute-done((bf16[128,10,1]{0,2,1:T(2,128)(2,1)S(1)}, bf16[128,10,1]{0,2,1:T(2,128)(2,1)S(1)}, u32[]{:S(2)}, u32[]{:S(2)}) %collective-permute-start.5) | collective-permute-done | bytes 2592 | tf_op jit(solution)/shard_map/ppermute | solution.py:24
  72.9 0.2 fusion.9
  73.1 0.8 %fusion.14 = bf16[64,8,16]{0,2,1:T(8,128)(2,1)} fusion(f32[8,16,64]{2,1,0:T(8,128)S(1)} %fusion.67, f32[8,16,64]{2,1,0:T(8,128)S(1)} %fusion.63, f32[8,16,64]{2,1,0:T(8,128)S(1)} %fusion.69, f32[8,16,64]{2,1,0:T(8,128)S(1)} %fusion.9, bf16[64,8,16]{0,2,1:T(8,128)(2,1)S(1)} %fusion.13, bf16[128,10,17]{0,2,1:T(8,128)(2,1)S(1)} %get-tuple-element.7, ...), kind=kOutput, calls=%fused_computation.31 | convolution fusion | flops 2154496 | bytes 360448 | tf_op jit(solution)/shard_map/co,crs->ors/dot_general | solution.py:43
  (58 shorter events, 2.8 us)
Async XLA Ops:
  0.6 21.3 %copy-start = (bf16[768,768]{1,0:T(8,128)(2,1)S(1)}, bf16[768,768]{1,0:T(8,128)(2,1)}, u32[]{:S(2)}) copy-start(bf16[768,768]{1,0:T(8,128)(2,1)} %param.14) | copy-start | bytes 3538948
  1.7 14.5 %copy-start.6 = (f32[768]{0:T(1024)S(1)}, f32[768]{0:T(1024)}, u32[]{:S(2)}) copy-start(f32[768]{0:T(1024)} %param.12) | copy-start | bytes 9220
  5.6 6.3 %collective-permute-start = (bf16[4,768]{1,0:T(4,128)(2,1)S(1)}, bf16[4,768]{1,0:T(4,128)(2,1)S(1)}, u32[]{:S(2)}, u32[]{:S(2)}) collective-permute-start(bf16[4,768]{1,0:T(4,128)(2,1)S(1)} %get-tuple-element.4), channel_id=1, source_target_pairs={{0,2},{2,4},{4,6},{6,8},{8,10},{10,12},{12,14},{1,3},{3,5},{5,7},{... | collective-permute-start | bytes 18440 | tf_op jit(solution)/shard_map/ppermute | solution.py:22
  10.4 5.5 %collective-permute-start.1 = (bf16[4,768]{1,0:T(4,128)(2,1)S(1)}, bf16[4,768]{1,0:T(4,128)(2,1)S(1)}, u32[]{:S(2)}, u32[]{:S(2)}) collective-permute-start(bf16[4,768]{1,0:T(4,128)(2,1)S(1)} %get-tuple-element.5), channel_id=1, source_target_pairs={{2,0},{4,2},{6,4},{8,6},{10,8},{12,10},{14,12},{3,1},{5,3},{7,5},{... | collective-permute-start | bytes 18440 | tf_op jit(solution)/shard_map/ppermute | solution.py:24
  11.9 4.7 %copy-start.2 = (bf16[3,768,384]{2,1,0:T(8,128)(2,1)S(1)}, bf16[3,768,384]{2,1,0:T(8,128)(2,1)}, u32[]{:S(2)}) copy-start(bf16[3,768,384]{2,1,0:T(8,128)(2,1)} %param.13) | copy-start | bytes 5308420
  21.9 3.3 %copy-start.1 = (bf16[1536,256]{1,0:T(8,128)(2,1)S(1)}, bf16[1536,256]{1,0:T(8,128)(2,1)}, u32[]{:S(2)}) copy-start(bf16[1536,256]{1,0:T(8,128)(2,1)} %param.16) | copy-start | bytes 2359300
  21.9 3.4 %copy-start.5 = (f32[1536]{0:T(1024)S(1)}, f32[1536]{0:T(1024)}, u32[]{:S(2)}) copy-start(f32[1536]{0:T(1024)} %param.15) | copy-start | bytes 18436
  21.9 30.3 %copy-start.7 = (f32[128]{0:T(128)S(1)}, f32[128]{0:T(128)}, u32[]{:S(2)}) copy-start(f32[128]{0:T(128)} %param.17) | copy-start | bytes 1540
  21.9 30.5 %copy-start.3 = (bf16[3,3,128,64]{2,3,1,0:T(8,128)(2,1)S(1)}, bf16[3,3,128,64]{2,3,1,0:T(8,128)(2,1)}, u32[]{:S(2)}) copy-start(bf16[3,3,128,64]{2,3,1,0:T(8,128)(2,1)} %param.18) | copy-start | bytes 442372
  25.5 34.0 %copy-start.4 = (bf16[3,3,128,64]{2,3,1,0:T(8,128)(2,1)S(1)}, bf16[3,3,128,64]{2,3,1,0:T(8,128)(2,1)}, u32[]{:S(2)}) copy-start(bf16[3,3,128,64]{2,3,1,0:T(8,128)(2,1)} %param.19) | copy-start | bytes 442372
  56.1 3.6 %collective-permute-start.2 = (bf16[128,1,16]{0,2,1:T(8,128)(2,1)S(1)}, bf16[128,1,16]{0,2,1:T(8,128)(2,1)S(1)}, u32[]{:S(2)}, u32[]{:S(2)}) collective-permute-start(bf16[128,1,16]{0,2,1:T(8,128)(2,1)S(1)} %get-tuple-element.10), channel_id=1, source_target_pairs={{0,4},{4,8},{8,12},{1,5},{5,9},{9,13},{2,6},{6,10},{10,14},{3,7},{... | collective-permute-start | bytes 12296 | tf_op jit(solution)/shard_map/ppermute | solution.py:22
  58.3 5.5 %collective-permute-start.3 = (bf16[128,1,16]{0,2,1:T(8,128)(2,1)S(1)}, bf16[128,1,16]{0,2,1:T(8,128)(2,1)S(1)}, u32[]{:S(2)}, u32[]{:S(2)}) collective-permute-start(bf16[128,1,16]{0,2,1:T(8,128)(2,1)S(1)} %get-tuple-element.11), channel_id=1, source_target_pairs={{4,0},{8,4},{12,8},{5,1},{9,5},{13,9},{6,2},{10,6},{14,10},{7,3},{... | collective-permute-start | bytes 12296 | tf_op jit(solution)/shard_map/ppermute | solution.py:24
  63.8 4.6 %collective-permute-start.4 = (bf16[128,10,1]{0,2,1:T(2,128)(2,1)S(1)}, bf16[128,10,1]{0,2,1:T(2,128)(2,1)S(1)}, u32[]{:S(2)}, u32[]{:S(2)}) collective-permute-start(bf16[128,10,1]{0,2,1:T(2,128)(2,1)S(1)} %get-tuple-element.8), channel_id=1, source_target_pairs={{0,2},{1,3},{4,6},{5,7},{8,10},{9,11},{12,14},{13,15},{16,18},{17,... | collective-permute-start | bytes 7688 | tf_op jit(solution)/shard_map/ppermute | solution.py:22
  66.8 5.5 %collective-permute-start.5 = (bf16[128,10,1]{0,2,1:T(2,128)(2,1)S(1)}, bf16[128,10,1]{0,2,1:T(2,128)(2,1)S(1)}, u32[]{:S(2)}, u32[]{:S(2)}) collective-permute-start(bf16[128,10,1]{0,2,1:T(2,128)(2,1)S(1)} %get-tuple-element.9), channel_id=1, source_target_pairs={{2,0},{3,1},{6,4},{7,5},{10,8},{11,9},{14,12},{15,13},{18,16},{19,... | collective-permute-start | bytes 7688 | tf_op jit(solution)/shard_map/ppermute | solution.py:24
where the time goes:
time: 74.2 us; the launch traced here: 73.8 us
  blocking collectives  35 us (47%)
  starting transfers between devices  13.8 us (19%)
  waiting for transfers between devices  12 us (16%)
  matrix products  7.84 us (11%)
  local copies, waits for them, and re-layouts  2.83 us (4%)
  other arithmetic  1.39 us (2%)
  between operations  0.97 us (1%)
    all_gather x1, blocking collectives, per_device(): lax.all_gather(factors, ('seq', 'section'), axis=0, tiled=True)  26.6 us
    ppermute x3, waiting for transfers between devices, padded(): lax.ppermute(head, axis, [((i + 1) % count, i) for i in range(ends)])  12 us
    ppermute x3, starting transfers between devices, padded(): lax.ppermute(tail, axis, [(i, (i + 1) % count) for i in range(ends)])  9.96 us
    ppermute x3, starting transfers between devices, padded(): lax.ppermute(head, axis, [((i + 1) % count, i) for i in range(ends)])  3.88 us
    dot_general x18, matrix products, pair_conv(): jnp.einsum('co,crs->ors', weight[shift_row, shift_col], window, preferred...  3.11 us
    all_gather x1, blocking collectives, per_device(): full_stem_output = lax.all_gather(stem_own, 'chan', axis=1, tiled=True)  2.49 us
    all_gather x1, blocking collectives, per_device(): lax.all_gather(halved, 'chan', axis=1, tiled=True)  2.09 us
    all_gather x1, blocking collectives, per_device(): mid_full = lax.all_gather(pair_mid, 'chan', axis=0, tiled=True)  1.99 us
  transfers between devices with their start and end apart: 6, of which 3 were waited for; matrix products, arithmetic and copies ran while one was open for 1% of the time, Pallas kernels for 0%

commit v1 on v0

--- a/solution.py
+++ b/solution.py
@@ -9,6 +9,18 @@
 POOL = 64
 DILATION_ROWS = 4
 epsilon = 1e-06
+
+
+def doubled_up(value, axis, dim):
+    ways, here, lap = (lax.axis_size(axis), lax.axis_index(axis), value.shape[dim])
+    line, have = (value, 1)
+    while have < ways:
+        line = jnp.concatenate(
+            [line, lax.ppermute(line, axis, [(d, (d - have) % ways) for d in range(ways)])],
+            axis=dim,
+        )
+        have = 2 * have
+    return jnp.roll(line, here * lap, axis=dim)
 
 
 def padded(cells, sides, width):
@@ -118,7 +130,7 @@
     row_anchor = lax.axis_index("seq") * tile_height
     col_anchor = lax.axis_index("section") * tile_width
     pair_own = pair_weight_one.shape[3]
-    every_token = lax.all_gather(factors, ("seq", "section"), axis=0, tiled=True)
+    every_token = doubled_up(factors, ("seq", "section"), 0)
     zero_padded = jnp.pad(every_token, ((1, 1), (0, 0)))
     row_factor = lax.dynamic_slice_in_dim(zero_padded, row_anchor, tile_height + 2, 0)[:, :PC]
     col_factor = lax.dynamic_slice_in_dim(zero_padded, col_anchor, tile_width + 2, 0)[:, PC:]

time: 74.2 us -> 63.6 us (0.86)
  blocking collectives: 35 us -> 8.39 us
  starting transfers between devices: 13.8 us -> 24.3 us
  waiting for transfers between devices: 12 us -> 17.5 us
    all_gather x1 -> x0, blocking collectives: 26.6 us -> none  [per_device(): lax.all_gather(factors, ('seq', 'section'), axis=0, tiled=True)]
    ppermute x0 -> x3, starting transfers between devices: none -> 7.7 us  [doubled_up(): lax.ppermute(line, axis, [(d, (d - have) % ways) for d in range(ways)])]
    ppermute x0 -> x3, waiting for transfers between devices: none -> 5.37 us  [doubled_up(): lax.ppermute(line, axis, [(d, (d - have) % ways) for d in range(ways)])]
    ppermute x3, starting transfers between devices: 9.96 us -> 12.8 us  [padded(): lax.ppermute(tail, axis, [(i, (i + 1) % count) for i in range(ends)])]
  transfers between devices with their start and end apart: 6 -> 9, of which waited for: 3 -> 6; matrix products, arithmetic and copies ran while one was open for 1% -> 1% of each run, Pallas kernels for 0% -> 0%
where the time goes in v1:
time: 63.6 us; the launch traced here: 63.3 us
  starting transfers between devices  24.3 us (38%)
  waiting for transfers between devices  17.5 us (28%)
  blocking collectives  8.39 us (13%)
  matrix products  7.84 us (12%)
  local copies, waits for them, and re-layouts  2.89 us (5%)
  other arithmetic  1.4 us (2%)
  between operations  0.98 us (2%)
    ppermute x3, starting transfers between devices, padded(): lax.ppermute(tail, axis, [(i, (i + 1) % count) for i in range(ends)])  12.8 us
    ppermute x3, waiting for transfers between devices, padded(): lax.ppermute(head, axis, [((i + 1) % count, i) for i in range(ends)])  12.1 us
    ppermute x3, starting transfers between devices, doubled_up(): lax.ppermute(line, axis, [(d, (d - have) % ways) for d in range(ways)])  7.7 us
    ppermute x3, waiting for transfers between devices, doubled_up(): lax.ppermute(line, axis, [(d, (d - have) % ways) for d in range(ways)])  5.37 us
    ppermute x3, starting transfers between devices, padded(): lax.ppermute(head, axis, [((i + 1) % count, i) for i in range(ends)])  3.88 us
    dot_general x18, matrix products, pair_conv(): jnp.einsum('co,crs->ors', weight[shift_row, shift_col], window, preferred...  3.11 us
    all_gather x1, blocking collectives, per_device(): full_stem_output = lax.all_gather(stem_own, 'chan', axis=1, tiled=True)  2.49 us
    all_gather x1, blocking collectives, per_device(): lax.all_gather(halved, 'chan', axis=1, tiled=True)  2.09 us
  transfers between devices with their start and end apart: 9, of which 6 were waited for; matrix products, arithmetic and copies ran while one was open for 1% of the time, Pallas kernels for 0%

profile of v1, /device:TPU:0, one launch (start us, length us, event | category | flops | bytes accessed | tf_op | source)
XLA Modules:
  0.0 63.3 jit_solution(9614648014909008688)
XLA Ops:
  0.7 1.0 %eq.25 = s32[512,16]{1,0:T(8,128)S(1)} reshape(s32[8192]{0:T(1024)} %param.10) | data formatting | bytes 65536 | tf_op jit(solution)/shard_map/eq | solution.py:88
  1.9 1.2 %convolution_convert_fusion = bf16[512,384]{1,0:T(8,128)(2,1)S(1)} fusion(s32[512,64]{0,1:T(8,128)S(1)} %eq.27, s32[64]{0:T(128)S(1)} %eq.29, bf16[64,768]{1,0:T(8,128)(2,1)} %param.11, s32[]{:T(128)S(6)} %select_n.29), kind=kOutput, calls=%fused_computation.7 | convolution fusion | flops 25395200 | bytes 573700 | tf_op jit(solution)/shard_map/dot_general | solution.py:95
  3.1 2.5 %all_gather.12 = bf16[512,768]{1,0:T(8,128)(2,1)S(1)} all-gather(bf16[512,384]{1,0:T(8,128)(2,1)S(1)} %convolution_convert_fusion), channel_id=1, replica_groups=mesh['groups'=2,'seq'=4,'section'=2,'chan'=2] {'chan'}, dimensions={1}, use_global_device_ids=true | all-gather | bytes 1179648 | tf_op jit(solution)/shard_map/all_gather | solution.py:96
  5.6 4.8 %collective-permute-start = (bf16[4,768]{1,0:T(4,128)(2,1)S(1)}, bf16[4,768]{1,0:T(4,128)(2,1)S(1)}, u32[]{:S(2)}, u32[]{:S(2)}) collective-permute-start(bf16[4,768]{1,0:T(4,128)(2,1)S(1)} %get-tuple-element.4), channel_id=1, source_target_pairs={{0,2},{2,4},{4,6},{6,8},{8,10},{10,12},{12,14},{1,3},{3,5},{5,7},{... | collective-permute-start | bytes 18440 | tf_op jit(solution)/shard_map/ppermute | solution.py:34
  10.4 1.3 %collective-permute-start.1 = (bf16[4,768]{1,0:T(4,128)(2,1)S(1)}, bf16[4,768]{1,0:T(4,128)(2,1)S(1)}, u32[]{:S(2)}, u32[]{:S(2)}) collective-permute-start(bf16[4,768]{1,0:T(4,128)(2,1)S(1)} %get-tuple-element.5), channel_id=1, source_target_pairs={{2,0},{4,2},{6,4},{8,6},{10,8},{12,10},{14,12},{3,1},{5,3},{7,5},{... | collective-permute-start | bytes 18440 | tf_op jit(solution)/shard_map/ppermute | solution.py:36
  11.8 4.1 %collective-permute-done.1 = bf16[4,768]{1,0:T(4,128)(2,1)S(1)} collective-permute-done((bf16[4,768]{1,0:T(4,128)(2,1)S(1)}, bf16[4,768]{1,0:T(4,128)(2,1)S(1)}, u32[]{:S(2)}, u32[]{:S(2)}) %collective-permute-start.1) | collective-permute-done | bytes 6176 | tf_op jit(solution)/shard_map/ppermute | solution.py:36
  15.9 0.3 fusion
  16.3 0.3 fusion.2
  16.6 0.6 fusion.33
  17.2 0.6 convolution_add_fusion.1
  17.8 0.8 %fusion.23 = bf16[512,384]{1,0:T(8,128)(2,1)S(1)} fusion(f32[512,384]{1,0:T(8,128)S(1)} %convolution_add_fusion.1, bf16[520,768]{1,0:T(8,128)(2,1)S(1)} %fusion.2, bf16[512,384]{1,0:T(8,128)(2,1)S(1)} %convolution_convert_fusion, bf16[3,768,384]{2,1,0:T(8,128)(2,1)S(1)} %copy-done.2), kind=kOutput, calls=%fused_computation.42 | convolution fusion | flops 304349184 | bytes 2949120 | tf_op jit(solution)/shard_map/dot_general | solution.py:101
  18.6 0.6 slice.172
  19.2 0.6 slice.173
  19.8 2.1 %all_gather.13 = bf16[256,768]{1,0:T(8,128)(2,1)S(1)} all-gather(bf16[256,384]{1,0:T(8,128)(2,1)S(1)} %max.3), channel_id=1, replica_groups=mesh['groups'=2,'seq'=4,'section'=2,'chan'=2] {'chan'}, dimensions={1}, use_global_device_ids=true | all-gather | bytes 589824 | tf_op jit(solution)/shard_map/all_gather | solution.py:111
  21.9 1.4 %convert_reduce_fusion = (f32[4,768]{1,0:T(4,128)S(1)}, bf16[256,768]{1,0:T(8,128)(2,1)}) fusion(bf16[256,768]{1,0:T(8,128)(2,1)S(1)} %all_gather.13, bf16[768,768]{1,0:T(8,128)(2,1)S(1)} %copy-done), kind=kOutput, calls=%fused_computation.55 | convolution fusion | flops 304149504 | bytes 1978368 | tf_op jit(solution)/shard_map/dot_general | solution.py:110
  23.3 1.8 %all_gather.14 = bf16[4,1536]{1,0:T(4,128)(2,1)S(1)} all-gather(bf16[4,768]{1,0:T(4,128)(2,1)S(1)} %multiply_convert_fusion), channel_id=1, replica_groups=mesh['groups'=2,'seq'=4,'section'=2,'chan'=2] {'chan'}, dimensions={1}, use_global_device_ids=true | all-gather | bytes 18432 | tf_op jit(solution)/shard_map/all_gather | solution.py:120
  25.3 0.2 convolution_convert_fusion.1
  25.5 2.8 %collective-permute-start.2 = (bf16[4,256]{1,0:T(4,128)(2,1)S(1)}, bf16[4,256]{1,0:T(4,128)(2,1)S(1)}, u32[]{:S(2)}, u32[]{:S(2)}) collective-permute-start(bf16[4,256]{1,0:T(4,128)(2,1)S(1)} %convolution_convert_fusion.1), channel_id=1, source_target_pairs={{0,14},{2,0},{4,2},{6,4},{8,6},{10,8},{12,10},{14,12},{1,15},{3,1}... | collective-permute-start | bytes 6152 | tf_op jit(solution)/shard_map/ppermute | solution.py:19
  28.3 1.3 %collective-permute-done.2 = bf16[4,256]{1,0:T(4,128)(2,1)S(1)} collective-permute-done((bf16[4,256]{1,0:T(4,128)(2,1)S(1)}, bf16[4,256]{1,0:T(4,128)(2,1)S(1)}, u32[]{:S(2)}, u32[]{:S(2)}) %collective-permute-start.2) | collective-permute-done | bytes 2080 | tf_op jit(solution)/shard_map/ppermute | solution.py:19
  29.6 3.2 %collective-permute-start.3 = (bf16[8,256]{1,0:T(8,128)(2,1)S(1)}, bf16[8,256]{1,0:T(8,128)(2,1)S(1)}, u32[]{:S(2)}, u32[]{:S(2)}) collective-permute-start(bf16[8,256]{1,0:T(8,128)(2,1)S(1)} %pad_maximum_fusion.6), channel_id=1, source_target_pairs={{0,12},{2,14},{4,0},{6,2},{8,4},{10,6},{12,8},{14,10},{1,13},{3,15... | collective-permute-start | bytes 12296 | tf_op jit(solution)/shard_map/ppermute | solution.py:19
  32.8 1.3 %collective-permute-done.3 = bf16[8,256]{1,0:T(8,128)(2,1)S(1)} collective-permute-done((bf16[8,256]{1,0:T(8,128)(2,1)S(1)}, bf16[8,256]{1,0:T(8,128)(2,1)S(1)}, u32[]{:S(2)}, u32[]{:S(2)}) %collective-permute-start.3) | collective-permute-done | bytes 4128 | tf_op jit(solution)/shard_map/ppermute | solution.py:19
  34.2 1.7 %collective-permute-start.4 = (bf16[16,256]{1,0:T(8,128)(2,1)S(1)}, bf16[16,256]{1,0:T(8,128)(2,1)S(1)}, u32[]{:S(2)}, u32[]{:S(2)}) collective-permute-start(bf16[16,256]{1,0:T(8,128)(2,1)S(1)} %pad_maximum_fusion.2), channel_id=1, source_target_pairs={{0,8},{2,10},{4,12},{6,14},{8,0},{10,2},{12,4},{14,6},{1,9},{3,11}... | collective-permute-start | bytes 24584 | tf_op jit(solution)/shard_map/ppermute | solution.py:19
  36.0 2.8 %collective-permute-done.4 = bf16[16,256]{1,0:T(8,128)(2,1)S(1)} collective-permute-done((bf16[16,256]{1,0:T(8,128)(2,1)S(1)}, bf16[16,256]{1,0:T(8,128)(2,1)S(1)}, u32[]{:S(2)}, u32[]{:S(2)}) %collective-permute-start.4) | collective-permute-done | bytes 8224 | tf_op jit(solution)/shard_map/ppermute | solution.py:19
  40.5 2.0 %all_gather.15 = bf16[128,8,16]{2,1,0:T(8,128)(2,1)S(1)} all-gather(bf16[64,8,16]{2,1,0:T(8,128)(2,1)S(1)} %copy.17), channel_id=1, replica_groups=mesh['groups'=2,'seq'=4,'section'=2,'chan'=2] {'chan'}, dimensions={0}, use_global_device_ids=true | all-gather | bytes 49152 | tf_op jit(solution)/shard_map/all_gather | solution.py:153
  42.5 0.2 copy.18
  42.7 3.7 %collective-permute-start.5 = (bf16[128,1,16]{0,2,1:T(8,128)(2,1)S(1)}, bf16[128,1,16]{0,2,1:T(8,128)(2,1)S(1)}, u32[]{:S(2)}, u32[]{:S(2)}) collective-permute-start(bf16[128,1,16]{0,2,1:T(8,128)(2,1)S(1)} %get-tuple-element.10), channel_id=1, source_target_pairs={{0,4},{4,8},{8,12},{1,5},{5,9},{9,13},{2,6},{6,10},{10,14},{3,7},{... | collective-permute-start | bytes 12296 | tf_op jit(solution)/shard_map/ppermute | solution.py:34
  46.4 1.3 %collective-permute-start.6 = (bf16[128,1,16]{0,2,1:T(8,128)(2,1)S(1)}, bf16[128,1,16]{0,2,1:T(8,128)(2,1)S(1)}, u32[]{:S(2)}, u32[]{:S(2)}) collective-permute-start(bf16[128,1,16]{0,2,1:T(8,128)(2,1)S(1)} %get-tuple-element.11), channel_id=1, source_target_pairs={{4,0},{8,4},{12,8},{5,1},{9,5},{13,9},{6,2},{10,6},{14,10},{7,3},{... | collective-permute-start | bytes 12296 | tf_op jit(solution)/shard_map/ppermute | solution.py:36
  47.9 4.0 %collective-permute-done.6 = bf16[128,1,16]{0,2,1:T(8,128)(2,1)S(1)} collective-permute-done((bf16[128,1,16]{0,2,1:T(8,128)(2,1)S(1)}, bf16[128,1,16]{0,2,1:T(8,128)(2,1)S(1)}, u32[]{:S(2)}, u32[]{:S(2)}) %collective-permute-start.6) | collective-permute-done | bytes 4128 | tf_op jit(solution)/shard_map/ppermute | solution.py:36
  51.9 4.3 %collective-permute-start.7 = (bf16[128,10,1]{0,2,1:T(2,128)(2,1)S(1)}, bf16[128,10,1]{0,2,1:T(2,128)(2,1)S(1)}, u32[]{:S(2)}, u32[]{:S(2)}) collective-permute-start(bf16[128,10,1]{0,2,1:T(2,128)(2,1)S(1)} %get-tuple-element.8), channel_id=1, source_target_pairs={{0,2},{1,3},{4,6},{5,7},{8,10},{9,11},{12,14},{13,15},{16,18},{17,... | collective-permute-start | bytes 7688 | tf_op jit(solution)/shard_map/ppermute | solution.py:34
  56.3 1.3 %collective-permute-start.8 = (bf16[128,10,1]{0,2,1:T(2,128)(2,1)S(1)}, bf16[128,10,1]{0,2,1:T(2,128)(2,1)S(1)}, u32[]{:S(2)}, u32[]{:S(2)}) collective-permute-start(bf16[128,10,1]{0,2,1:T(2,128)(2,1)S(1)} %get-tuple-element.9), channel_id=1, source_target_pairs={{2,0},{3,1},{6,4},{7,5},{10,8},{11,9},{14,12},{15,13},{18,16},{19,... | collective-permute-start | bytes 7688 | tf_op jit(solution)/shard_map/ppermute | solution.py:36
  57.8 4.0 %collective-permute-done.8 = bf16[128,10,1]{0,2,1:T(2,128)(2,1)S(1)} collective-permute-done((bf16[128,10,1]{0,2,1:T(2,128)(2,1)S(1)}, bf16[128,10,1]{0,2,1:T(2,128)(2,1)S(1)}, u32[]{:S(2)}, u32[]{:S(2)}) %collective-permute-start.8) | collective-permute-done | bytes 2592 | tf_op jit(solution)/shard_map/ppermute | solution.py:36
  62.5 0.8 %fusion.14 = bf16[64,8,16]{0,2,1:T(8,128)(2,1)} fusion(f32[8,16,64]{2,1,0:T(8,128)S(1)} %fusion.66, f32[8,16,64]{2,1,0:T(8,128)S(1)} %fusion.62, f32[8,16,64]{2,1,0:T(8,128)S(1)} %fusion.68, f32[8,16,64]{2,1,0:T(8,128)S(1)} %fusion.9, bf16[64,8,16]{0,2,1:T(8,128)(2,1)S(1)} %fusion.13, bf16[128,10,17]{0,2,1:T(8,128)(2,1)S(1)} %get-tuple-element.7, ...), kind=kOutput, calls=%fused_computation.31 | convolution fusion | flops 2154496 | bytes 360448 | tf_op jit(solution)/shard_map/co,crs->ors/dot_general | solution.py:55
  (66 shorter events, 3.6 us)
Async XLA Ops:
  0.6 21.3 %copy-start = (bf16[768,768]{1,0:T(8,128)(2,1)S(1)}, bf16[768,768]{1,0:T(8,128)(2,1)}, u32[]{:S(2)}) copy-start(bf16[768,768]{1,0:T(8,128)(2,1)} %param.14) | copy-start | bytes 3538948
  1.7 14.5 %copy-start.6 = (f32[768]{0:T(1024)S(1)}, f32[768]{0:T(1024)}, u32[]{:S(2)}) copy-start(f32[768]{0:T(1024)} %param.12) | copy-start | bytes 9220
  5.6 6.2 %collective-permute-start = (bf16[4,768]{1,0:T(4,128)(2,1)S(1)}, bf16[4,768]{1,0:T(4,128)(2,1)S(1)}, u32[]{:S(2)}, u32[]{:S(2)}) collective-permute-start(bf16[4,768]{1,0:T(4,128)(2,1)S(1)} %get-tuple-element.4), channel_id=1, source_target_pairs={{0,2},{2,4},{4,6},{6,8},{8,10},{10,12},{12,14},{1,3},{3,5},{5,7},{... | collective-permute-start | bytes 18440 | tf_op jit(solution)/shard_map/ppermute | solution.py:34
  10.4 5.5 %collective-permute-start.1 = (bf16[4,768]{1,0:T(4,128)(2,1)S(1)}, bf16[4,768]{1,0:T(4,128)(2,1)S(1)}, u32[]{:S(2)}, u32[]{:S(2)}) collective-permute-start(bf16[4,768]{1,0:T(4,128)(2,1)S(1)} %get-tuple-element.5), channel_id=1, source_target_pairs={{2,0},{4,2},{6,4},{8,6},{10,8},{12,10},{14,12},{3,1},{5,3},{7,5},{... | collective-permute-start | bytes 18440 | tf_op jit(solution)/shard_map/ppermute | solution.py:36
  11.7 4.9 %copy-start.2 = (bf16[3,768,384]{2,1,0:T(8,128)(2,1)S(1)}, bf16[3,768,384]{2,1,0:T(8,128)(2,1)}, u32[]{:S(2)}) copy-start(bf16[3,768,384]{2,1,0:T(8,128)(2,1)} %param.13) | copy-start | bytes 5308420
  21.9 3.3 %copy-start.1 = (bf16[1536,256]{1,0:T(8,128)(2,1)S(1)}, bf16[1536,256]{1,0:T(8,128)(2,1)}, u32[]{:S(2)}) copy-start(bf16[1536,256]{1,0:T(8,128)(2,1)} %param.16) | copy-start | bytes 2359300
  21.9 3.4 %copy-start.5 = (f32[1536]{0:T(1024)S(1)}, f32[1536]{0:T(1024)}, u32[]{:S(2)}) copy-start(f32[1536]{0:T(1024)} %param.15) | copy-start | bytes 18436
  21.9 17.0 %copy-start.7 = (f32[128]{0:T(128)S(1)}, f32[128]{0:T(128)}, u32[]{:S(2)}) copy-start(f32[128]{0:T(128)} %param.17) | copy-start | bytes 1540
  21.9 17.1 %copy-start.3 = (bf16[3,3,128,64]{2,3,1,0:T(8,128)(2,1)S(1)}, bf16[3,3,128,64]{2,3,1,0:T(8,128)(2,1)}, u32[]{:S(2)}) copy-start(bf16[3,3,128,64]{2,3,1,0:T(8,128)(2,1)} %param.18) | copy-start | bytes 442372
  25.5 22.2 %copy-start.4 = (bf16[3,3,128,64]{2,3,1,0:T(8,128)(2,1)S(1)}, bf16[3,3,128,64]{2,3,1,0:T(8,128)(2,1)}, u32[]{:S(2)}) copy-start(bf16[3,3,128,64]{2,3,1,0:T(8,128)(2,1)} %param.19) | copy-start | bytes 442372
  25.5 4.1 %collective-permute-start.2 = (bf16[4,256]{1,0:T(4,128)(2,1)S(1)}, bf16[4,256]{1,0:T(4,128)(2,1)S(1)}, u32[]{:S(2)}, u32[]{:S(2)}) collective-permute-start(bf16[4,256]{1,0:T(4,128)(2,1)S(1)} %convolution_convert_fusion.1), channel_id=1, source_target_pairs={{0,14},{2,0},{4,2},{6,4},{8,6},{10,8},{12,10},{14,12},{1,15},{3,1}... | collective-permute-start | bytes 6152 | tf_op jit(solution)/shard_map/ppermute | solution.py:19
  29.6 4.5 %collective-permute-start.3 = (bf16[8,256]{1,0:T(8,128)(2,1)S(1)}, bf16[8,256]{1,0:T(8,128)(2,1)S(1)}, u32[]{:S(2)}, u32[]{:S(2)}) collective-permute-start(bf16[8,256]{1,0:T(8,128)(2,1)S(1)} %pad_maximum_fusion.6), channel_id=1, source_target_pairs={{0,12},{2,14},{4,0},{6,2},{8,4},{10,6},{12,8},{14,10},{1,13},{3,15... | collective-permute-start | bytes 12296 | tf_op jit(solution)/shard_map/ppermute | solution.py:19
  34.2 4.5 %collective-permute-start.4 = (bf16[16,256]{1,0:T(8,128)(2,1)S(1)}, bf16[16,256]{1,0:T(8,128)(2,1)S(1)}, u32[]{:S(2)}, u32[]{:S(2)}) collective-permute-start(bf16[16,256]{1,0:T(8,128)(2,1)S(1)} %pad_maximum_fusion.2), channel_id=1, source_target_pairs={{0,8},{2,10},{4,12},{6,14},{8,0},{10,2},{12,4},{14,6},{1,9},{3,11}... | collective-permute-start | bytes 24584 | tf_op jit(solution)/shard_map/ppermute | solution.py:19
  42.7 5.2 %collective-permute-start.5 = (bf16[128,1,16]{0,2,1:T(8,128)(2,1)S(1)}, bf16[128,1,16]{0,2,1:T(8,128)(2,1)S(1)}, u32[]{:S(2)}, u32[]{:S(2)}) collective-permute-start(bf16[128,1,16]{0,2,1:T(8,128)(2,1)S(1)} %get-tuple-element.10), channel_id=1, source_target_pairs={{0,4},{4,8},{8,12},{1,5},{5,9},{9,13},{2,6},{6,10},{10,14},{3,7},{... | collective-permute-start | bytes 12296 | tf_op jit(solution)/shard_map/ppermute | solution.py:34
  46.4 5.5 %collective-permute-start.6 = (bf16[128,1,16]{0,2,1:T(8,128)(2,1)S(1)}, bf16[128,1,16]{0,2,1:T(8,128)(2,1)S(1)}, u32[]{:S(2)}, u32[]{:S(2)}) collective-permute-start(bf16[128,1,16]{0,2,1:T(8,128)(2,1)S(1)} %get-tuple-element.11), channel_id=1, source_target_pairs={{4,0},{8,4},{12,8},{5,1},{9,5},{13,9},{6,2},{10,6},{14,10},{7,3},{... | collective-permute-start | bytes 12296 | tf_op jit(solution)/shard_map/ppermute | solution.py:36
  51.9 5.9 %collective-permute-start.7 = (bf16[128,10,1]{0,2,1:T(2,128)(2,1)S(1)}, bf16[128,10,1]{0,2,1:T(2,128)(2,1)S(1)}, u32[]{:S(2)}, u32[]{:S(2)}) collective-permute-start(bf16[128,10,1]{0,2,1:T(2,128)(2,1)S(1)} %get-tuple-element.8), channel_id=1, source_target_pairs={{0,2},{1,3},{4,6},{5,7},{8,10},{9,11},{12,14},{13,15},{16,18},{17,... | collective-permute-start | bytes 7688 | tf_op jit(solution)/shard_map/ppermute | solution.py:34
  56.3 5.5 %collective-permute-start.8 = (bf16[128,10,1]{0,2,1:T(2,128)(2,1)S(1)}, bf16[128,10,1]{0,2,1:T(2,128)(2,1)S(1)}, u32[]{:S(2)}, u32[]{:S(2)}) collective-permute-start(bf16[128,10,1]{0,2,1:T(2,128)(2,1)S(1)} %get-tuple-element.9), channel_id=1, source_target_pairs={{2,0},{3,1},{6,4},{7,5},{10,8},{11,9},{14,12},{15,13},{18,16},{19,... | collective-permute-start | bytes 7688 | tf_op jit(solution)/shard_map/ppermute | solution.py:36
